TPU v7x, 128 devices: a whole 4x4x4 slice. The times are simulated.
128 devices in a mesh: row: 16 (over z, x_hi, core), col: 8 (over x_lo, y).
Axes of the slice: x: 4 (x_hi: 2, x_lo: 2; x = x_hi * 2 + x_lo), y: 4, z: 4, core: 2. Of those that a mesh axis runs over, the one named last changes fastest.
Arguments:
- stored: bfloat16 [1024, 51200], P(('row', 'col')), may hold values from -24 to 24
- integrals: bfloat16 [51200, 25600], P('row', 'col'), may hold values from -0.02734375 to 0.02734375
- layout: int32 [1024], replicated, may hold values from 0 to 1023, each once
- partner: int32 [1024], replicated, may hold values from 0 to 1023, as said below
Outputs:
- residual_out: bfloat16 [1024, 25600], P('row', 'col')
Inputs may be any that keep to these rules, and one draw needn't show every extreme that they name: partner is an involution without fixed points: partner[p] != p and partner[partner[p]] = p. `layout`: each slab pair stands in exactly one stored row.
All inputs are finite; a program needn't handle non-finite values.
Results may differ from a plain program's by a relative error of at most 0.001.
Values may be sent and summed in bfloat16 or wider, within the bound.
A program may use at most 128 MiB of HBM per device.

v0:
```python
import jax
import jax.numpy as jnp
from jax import lax
from jax.sharding import PartitionSpec as P


def per_device(stored, integrals, layout, partner):
    local_rows = stored.shape[0]
    n_row = lax.axis_size("row")
    n_col = lax.axis_size("col")
    total = local_rows * n_row * n_col
    regrouped = lax.all_to_all(stored, "row", split_axis=1, concat_axis=0, tiled=True)
    partial_sums = jnp.dot(
        lax.all_gather(regrouped, "col", axis=0, tiled=True),
        integrals,
        preferred_element_type=jnp.float32,
    )
    place = jnp.arange(total, dtype=jnp.int32)
    group_size = n_row * local_rows
    source_col = place // group_size
    remain = place % group_size
    source_row = remain // local_rows
    offset = remain % local_rows
    stored_index = (source_row * n_col + source_col) * local_rows + offset
    where_global = jnp.zeros((total,), jnp.int32).at[layout[stored_index]].set(place)
    difference = partial_sums[where_global] - partial_sums[where_global[partner]]
    return lax.psum_scatter(difference, "row", scatter_dimension=0, tiled=True).astype(jnp.bfloat16)


def solution(mesh):
    return jax.shard_map(
        per_device,
        mesh=mesh,
        in_specs=(P(("row", "col"), None), P("row", "col"), P(), P()),
        out_specs=P("row", "col"),
        check_vma=False,
    )
```

profile of v0, /device:TPU:1, one launch (start us, length us, event | category | flops | bytes accessed | tf_op | source)
XLA Modules:
  0.0 313.7 jit_solution(5771795690259070240)
XLA Ops:
  6.5 0.0 copy-start
  6.5 0.0 all-gather.2.cloned.1.call-start
  6.5 24.0 %all_to_all.19 = bf16[8,16,3200]{2,0,1:T(8,128)(2,1)} all-to-all(bf16[8,16,3200]{2,0,1:T(8,128)(2,1)} %bitcast.13), channel_id=1, replica_groups=mesh['row'=16,'col'=8] {'row'}, dimensions={1} | all-to-all | bytes 1638400 | tf_op jit(solution)/shard_map/all_to_all | solution.py:12
  30.6 0.0 all-gather.2.cloned.1.call-update
  30.6 0.0 reduce-scatter.2.cloned.1.call-start
  30.7 0.0 copy-done
  30.7 4.5 %gather_fusion = s32[1024]{0:T(1024)S(1)} fusion(s32[1024]{0:T(1024)S(1)} %copy-done, s32[1024]{0:T(1024)S(1)} %broadcast_clamp_fusion.1), kind=kCustom, calls=%fused_computation | custom fusion | bytes 12288 | tf_op jit(solution)/shard_map/gather | solution.py:25
  35.3 4.3 %scatter_custom_fusion = s32[1024]{0:T(1024)S(1)} fusion(s32[1024]{0:T(1024)S(1)} %bitcast.18, s32[1024]{0:T(1024)S(1)} %iota.7, s32[]{:T(128)} %constant.45.clone.1), kind=kCustom, calls=%fused_computation.27 | custom fusion | bytes 4100 | tf_op jit(solution)/shard_map/scatter | solution.py:25
  39.6 0.7 fusion.4
  40.3 4.5 %gather_fusion.2 = s32[1024]{0:T(1024)S(1)} fusion(s32[1024]{0:T(1024)S(1)} %scatter_custom_fusion, s32[1024]{0:T(1024)S(1)} %fusion.4), kind=kCustom, calls=%fused_computation.2 | custom fusion | bytes 12288 | tf_op jit(solution)/shard_map/gather | solution.py:26
  44.8 57.9 %all-gather.2.cloned.1.call-done = bf16[1024,3200]{1,0:T(8,128)(2,1)} async-done(((bf16[128,3200]{1,0:T(8,128)(2,1)}), bf16[1024,3200]{1,0:T(8,128)(2,1)}) %all-gather.2.cloned.1.call-update) | async-done | bytes 6553616 | tf_op jit(solution)/shard_map/all_gather | solution.py:14
  102.7 30.6 %fusion.7 = f32[1024,3200]{1,0:T(8,128)} fusion(bf16[1024,3200]{1,0:T(8,128)(2,1)} %all-gather.2.cloned.1.call-done, bf16[3200,3200]{1,0:T(8,128)(2,1)} %param.5), kind=kOutput, calls=%fused_computation.29 | convolution fusion | flops 20971520000 | bytes 40140800 | tf_op jit(solution)/shard_map/dot_general | solution.py:13
  133.3 17.1 %gather_fusion.3 = f32[1024,3200]{1,0:T(8,128)} fusion(f32[1024,3200]{1,0:T(8,128)} %fusion.7, s32[1024]{0:T(1024)S(1)} %broadcast_clamp_fusion), kind=kCustom, calls=%fused_computation.3 | custom fusion | bytes 26218496 | tf_op jit(solution)/shard_map/gather | solution.py:26
  150.4 17.1 %gather_fusion.1 = f32[1024,3200]{1,0:T(8,128)} fusion(f32[1024,3200]{1,0:T(8,128)} %fusion.7, s32[1024]{0:T(1024)S(1)} %fusion.3), kind=kCustom, calls=%fused_computation.1 | custom fusion | bytes 26218496 | tf_op jit(solution)/shard_map/gather | solution.py:26
  167.5 0.0 copy-start.1
  167.5 14.4 %sub.15 = f32[1024,3200]{1,0:T(8,128)} subtract(f32[1024,3200]{1,0:T(8,128)} %gather_fusion.1, f32[1024,3200]{1,0:T(8,128)} %gather_fusion.3) | non-fusion elementwise | flops 3276800 | bytes 39321600 | tf_op jit(solution)/shard_map/sub | solution.py:26
  181.8 0.0 reduce-scatter.2.cloned.1.call-update
  181.8 123.1 %reduce-scatter.2.cloned.1.call-done = f32[64,3200]{1,0:T(8,128)} async-done(((f32[1024,3200]{1,0:T(8,128)}), f32[64,3200]{1,0:T(8,128)}) %reduce-scatter.2.cloned.1.call-update) | async-done | bytes 819216 | tf_op jit(solution)/shard_map/reduce_scatter | solution.py:27
  305.0 1.9 convert_element_type.3
  306.9 0.0 copy-done.1
  (7 shorter events, 0.1 us)
Async XLA Ops:
  6.5 24.2 %copy-start = (s32[1024]{0:T(1024)S(1)}, s32[1024]{0:T(1024)}, u32[]{:S(2)}) copy-start(s32[1024]{0:T(1024)} %param.6) | copy-start | bytes 12292
  6.5 96.2 %all-gather.2.cloned.1.call-start = ((), (), s32[]{:S(2)}) async-start(), calls=%async_computation.2 | async-start | bytes 7372800 | tf_op jit(solution)/shard_map/all_gather | solution.py:14
  30.6 274.4 %reduce-scatter.2.cloned.1.call-start = ((), (), s32[]{:S(2)}) async-start(), calls=%async_computation.3 | async-start | bytes 13926400 | tf_op jit(solution)/shard_map/reduce_scatter | solution.py:27
  167.5 139.4 %copy-start.1 = (s32[1024]{0:T(1024)S(1)}, s32[1024]{0:T(1024)}, u32[]{:S(2)}) copy-start(s32[1024]{0:T(1024)} %param.6) | copy-start | bytes 12292
Sparse Core Ops, SparseCore 0:
  30.7 71.9 all-gather.1
  182.0 122.9 reduce-scatter.1
where the time goes:
time: 314 us
  waiting for transfers between devices  181 us (58%)
  local copies, waits for them, and re-layouts  47.5 us (15%)
  matrix products  30.6 us (10%)
  blocking collectives  24 us (8%)
  other arithmetic  17.1 us (5%)
  between operations  13.5 us (4%)
    reduce_scatter x1, waiting for transfers between devices, per_device(): lax.psum_scatter(difference, 'row', scatter_dimension=0, tiled=True)  123 us
    all_gather x1, waiting for transfers between devices, per_device(): lax.all_gather(regrouped, 'col', axis=0, tiled=True)  57.9 us
    dot_general x1, matrix products, per_device(): jnp.dot(lax.all_gather(regrouped, 'col', axis=0, tiled=True), integrals,...  30.6 us
    all_to_all x1, blocking collectives, per_device(): lax.all_to_all(stored, 'row', split_axis=1, concat_axis=0, tiled=True)  24 us
    gather x1, local copies, waits for them, and re-layouts, per_device(): partial_sums[where_global[partner]]  17.1 us
    gather x1, local copies, waits for them, and re-layouts, per_device(): partial_sums[where_global] - partial_sums[where_global[partner]]  17.1 us
    sub x1, other arithmetic, per_device(): partial_sums[where_global] - partial_sums[where_global[partner]]  14.4 us
  transfers between devices with their start and end apart: 2, of which 2 were waited for; matrix products, arithmetic and copies ran while one was open for 5% of the time, Pallas kernels for 0%

commit v1 on v0

--- a/solution.py
+++ b/solution.py
@@ -11,7 +11,9 @@
     total = local_rows * n_row * n_col
     regrouped = lax.all_to_all(stored, "row", split_axis=1, concat_axis=0, tiled=True)
     partial_sums = jnp.dot(
-        lax.all_gather(regrouped, "col", axis=0, tiled=True),
+        jnp.concatenate(
+            lax.all_to_all(jnp.stack([regrouped] * lax.axis_size("col")), "col", 0, 0), axis=0
+        ),
         integrals,
         preferred_element_type=jnp.float32,
     )

time: 314 us -> 322 us (1.025)
  starting transfers between devices: 0.04 us -> 4.82 us
  local copies, waits for them, and re-layouts: 47.5 us -> 51.1 us
    all_to_all x0 -> x1, waiting for transfers between devices: none -> 60.5 us  [per_device(): lax.all_to_all(jnp.stack([regrouped] * lax.axis_size('col')), 'col', 0, 0)]
    all_gather x1 -> x0, waiting for transfers between devices: 57.9 us -> none  [per_device(): lax.all_gather(regrouped, 'col', axis=0, tiled=True)]
    all_to_all x0 -> x1, starting transfers between devices: none -> 4.78 us  [per_device(): lax.all_to_all(jnp.stack([regrouped] * lax.axis_size('col')), 'col', 0, 0)]
    another operation x0 -> x1, local copies, waits for them, and re-layouts: none -> 3.53 us  [per_device(): jnp.stack([regrouped] * lax.axis_size('col'))]
  transfers between devices with their start and end apart: 2 -> 2, of which waited for: 2 -> 2; matrix products, arithmetic and copies ran while one was open for 5% -> 4% of each run, Pallas kernels for 0% -> 0%
where the time goes in v1:
time: 322 us
  waiting for transfers between devices  181 us (56%)
  local copies, waits for them, and re-layouts  51.1 us (16%)
  matrix products  30.6 us (10%)
  blocking collectives  23.9 us (7%)
  other arithmetic  16.4 us (5%)
  between operations  13.5 us (4%)
  starting transfers between devices  4.82 us (1%)
    reduce_scatter x1, waiting for transfers between devices, per_device(): lax.psum_scatter(difference, 'row', scatter_dimension=0, tiled=True)  121 us
    all_to_all x1, waiting for transfers between devices, per_device(): lax.all_to_all(jnp.stack([regrouped] * lax.axis_size('col')), 'col', 0, 0)  60.5 us
    dot_general x1, matrix products, per_device(): jnp.dot(jnp.concatenate(lax.all_to_all(jnp.stack([regrouped] * lax.axis_s...  30.6 us
    all_to_all x1, blocking collectives, per_device(): lax.all_to_all(stored, 'row', split_axis=1, concat_axis=0, tiled=True)  23.9 us
    gather x1, local copies, waits for them, and re-layouts, per_device(): partial_sums[where_global[partner]]  17.1 us
    gather x1, local copies, waits for them, and re-layouts, per_device(): partial_sums[where_global] - partial_sums[where_global[partner]]  17.1 us
    sub x1, other arithmetic, per_device(): partial_sums[where_global] - partial_sums[where_global[partner]]  14.4 us
  transfers between devices with their start and end apart: 2, of which 2 were waited for; matrix products, arithmetic and copies ran while one was open for 4% of the time, Pallas kernels for 0%

profile of v1, /device:TPU:1, one launch (start us, length us, event | category | flops | bytes accessed | tf_op | source)
XLA Modules:
  0.0 321.7 jit_solution(7081316567158587425)
XLA Ops:
  6.5 0.0 copy-start
  6.5 0.0 copy-start.2
  6.5 23.9 %all_to_all.21 = bf16[8,16,3200]{2,0,1:T(8,128)(2,1)S(1)} all-to-all(bf16[8,16,3200]{2,0,1:T(8,128)(2,1)} %bitcast.14), channel_id=1, replica_groups=mesh['row'=16,'col'=8] {'row'}, dimensions={1} | all-to-all | bytes 1638400 | tf_op jit(solution)/shard_map/all_to_all | solution.py:12
  30.5 3.5 %stack.5 = bf16[8,128,3200]{2,1,0:T(8,128)(2,1)} broadcast(bf16[128,3200]{1,0:T(8,128)(2,1)S(1)} %bitcast.13), dimensions={1,2} | broadcast | bytes 7372800 | tf_op jit(solution)/shard_map/stack | solution.py:15
  34.0 4.8 %all-to-all-start.1 = ((bf16[8,128,3200]{2,1,0:T(8,128)(2,1)}), bf16[8,128,3200]{2,1,0:T(8,128)(2,1)}, u32[]{:S(2)}, u32[]{:S(2)}) async-start(bf16[8,128,3200]{2,1,0:T(8,128)(2,1)} %stack.5), calls=%async_computation.1 | async-start | bytes 13107200 | tf_op jit(solution)/shard_map/all_to_all | solution.py:15
  38.8 0.0 reduce-scatter.2.cloned.1.call-start
  38.9 0.0 copy-done
  38.9 4.5 %gather_fusion = s32[1024]{0:T(1024)S(1)} fusion(s32[1024]{0:T(1024)S(1)} %copy-done, s32[1024]{0:T(1024)S(1)} %broadcast_clamp_fusion.1), kind=kCustom, calls=%fused_computation | custom fusion | bytes 12288 | tf_op jit(solution)/shard_map/gather | solution.py:27
  43.5 4.3 %scatter_custom_fusion = s32[1024]{0:T(1024)S(1)} fusion(s32[1024]{0:T(1024)S(1)} %bitcast.19, s32[1024]{0:T(1024)S(1)} %iota.7, s32[]{:T(128)} %constant.45.clone.1), kind=kCustom, calls=%fused_computation.27 | custom fusion | bytes 4100 | tf_op jit(solution)/shard_map/scatter | solution.py:27
  47.8 0.0 copy-done.2
  47.8 4.5 %gather_fusion.2 = s32[1024]{0:T(1024)S(1)} fusion(s32[1024]{0:T(1024)S(1)} %scatter_custom_fusion, s32[1024]{0:T(1024)S(1)} %fusion.4), kind=kCustom, calls=%fused_computation.2 | custom fusion | bytes 12288 | tf_op jit(solution)/shard_map/gather | solution.py:28
  52.4 60.5 %all-to-all-done.1 = bf16[8,128,3200]{2,1,0:T(8,128)(2,1)} async-done(((bf16[8,128,3200]{2,1,0:T(8,128)(2,1)}), bf16[8,128,3200]{2,1,0:T(8,128)(2,1)}, u32[]{:S(2)}, u32[]{:S(2)}) %all-to-all-start.1) | async-done | bytes 6553632 | tf_op jit(solution)/shard_map/all_to_all | solution.py:15
  112.9 30.6 %fusion.7 = f32[1024,3200]{1,0:T(8,128)} fusion(bf16[1024,3200]{1,0:T(8,128)(2,1)} %bitcast.3, bf16[3200,3200]{1,0:T(8,128)(2,1)} %param.5), kind=kOutput, calls=%fused_computation.29 | convolution fusion | flops 20971520000 | bytes 40140800 | tf_op jit(solution)/shard_map/dot_general | solution.py:13
  143.5 17.1 %gather_fusion.3 = f32[1024,3200]{1,0:T(8,128)} fusion(f32[1024,3200]{1,0:T(8,128)} %fusion.7, s32[1024]{0:T(1024)S(1)} %broadcast_clamp_fusion), kind=kCustom, calls=%fused_computation.3 | custom fusion | bytes 26218496 | tf_op jit(solution)/shard_map/gather | solution.py:28
  160.6 17.1 %gather_fusion.1 = f32[1024,3200]{1,0:T(8,128)} fusion(f32[1024,3200]{1,0:T(8,128)} %fusion.7, s32[1024]{0:T(1024)S(1)} %fusion.3), kind=kCustom, calls=%fused_computation.1 | custom fusion | bytes 26218496 | tf_op jit(solution)/shard_map/gather | solution.py:28
  177.6 0.0 copy-start.1
  177.7 14.4 %sub.15 = f32[1024,3200]{1,0:T(8,128)} subtract(f32[1024,3200]{1,0:T(8,128)} %gather_fusion.1, f32[1024,3200]{1,0:T(8,128)} %gather_fusion.3) | non-fusion elementwise | flops 3276800 | bytes 39321600 | tf_op jit(solution)/shard_map/sub | solution.py:28
  192.0 0.0 reduce-scatter.2.cloned.1.call-update
  192.0 120.9 %reduce-scatter.2.cloned.1.call-done = f32[64,3200]{1,0:T(8,128)} async-done(((f32[1024,3200]{1,0:T(8,128)}), f32[64,3200]{1,0:T(8,128)}) %reduce-scatter.2.cloned.1.call-update) | async-done | bytes 819216 | tf_op jit(solution)/shard_map/reduce_scatter | solution.py:29
  312.9 1.9 convert_element_type.3
  314.9 0.0 copy-done.1
  (8 shorter events, 0.1 us)
Async XLA Ops:
  6.5 32.4 %copy-start = (s32[1024]{0:T(1024)S(1)}, s32[1024]{0:T(1024)}, u32[]{:S(2)}) copy-start(s32[1024]{0:T(1024)} %param.6) | copy-start | bytes 12292
  6.5 41.2 %copy-start.2 = (s32[1024]{0:T(1024)S(1)}, s32[1024]{0:T(1024)}, u32[]{:S(2)}) copy-start(s32[1024]{0:T(1024)} %param.7) | copy-start | bytes 12292
  34.0 78.9 %all-to-all-start.1 = ((bf16[8,128,3200]{2,1,0:T(8,128)(2,1)}), bf16[8,128,3200]{2,1,0:T(8,128)(2,1)}, u32[]{:S(2)}, u32[]{:S(2)}) async-start(bf16[8,128,3200]{2,1,0:T(8,128)(2,1)} %stack.5), calls=%async_computation.1 | async-start | bytes 13107200 | tf_op jit(solution)/shard_map/all_to_all | solution.py:15
  38.8 274.1 %reduce-scatter.2.cloned.1.call-start = ((), (), s32[]{:S(2)}) async-start(), calls=%async_computation.3 | async-start | bytes 13926400 | tf_op jit(solution)/shard_map/reduce_scatter | solution.py:29
  177.6 137.2 %copy-start.1 = (s32[1024]{0:T(1024)S(1)}, s32[1024]{0:T(1024)}, u32[]{:S(2)}) copy-start(s32[1024]{0:T(1024)} %param.6) | copy-start | bytes 12292
Sparse Core Ops, SparseCore 0:
  192.2 120.7 reduce-scatter.1
